TPU v7x, 256 devices: a whole 4x4x8 slice. The times are simulated.
256 devices in a mesh: seq: 32 (over y, x, core), chan: 8 (over z).
Axes of the slice: x: 4, y: 4, z: 8, core: 2. Of those that a mesh axis runs over, the one named last changes fastest.
Arguments:
- conv_in: bfloat16 [32, 512, 512], P(None, 'seq', 'chan'), may hold values from -4 to 4
- conv_gate: bfloat16 [32, 512, 512], P(None, 'seq', 'chan'), may hold values from -4 to 4
- long_filter: float32 [32, 512, 512], P(None, 'seq', 'chan'), may hold values from -1.1 to 1.1
- skip_gain: float32 [512], P('chan'), may hold values from 0.5 to 1.5
- queries: bfloat16 [32, 512, 1024], P(None, 'seq', 'chan'), may hold values from -40 to 40
- keys_in: bfloat16 [32, 512, 1024], P(None, 'seq', 'chan'), may hold values from -40 to 40
- w_value: bfloat16 [512, 1024], P(None, 'chan'), may hold values from -0.25 to 0.25
Outputs:
- conv_out: bfloat16 [32, 512, 512], P(None, 'seq', 'chan')
- attended: bfloat16 [32, 512, 1024], P(None, 'seq', 'chan')
All inputs are finite; a program needn't handle non-finite values.
Results may differ from a plain program's by a relative error of at most 0.015.
Values may be sent and summed in bfloat16 or wider, within the bound.
A program may use at most 64 MiB of HBM per device.

v0:
```python
import math
import jax
import jax.numpy as jnp
from jax import lax
from jax.sharding import PartitionSpec as P


def mixdot(form, left, right):
    return jnp.einsum(form, left, right, precision=lax.Precision.HIGHEST)


def channel_convolve(signal, long_filter):
    moved_sig, moved_tap = (
        lax.all_to_all(
            signal.astype(jnp.bfloat16), "seq", split_axis=2, concat_axis=1, tiled=True
        ).astype(signal.dtype),
        lax.all_to_all(
            long_filter.astype(jnp.bfloat16), "seq", split_axis=2, concat_axis=1, tiled=True
        ).astype(long_filter.dtype),
    )
    blocks = moved_sig.shape[0]
    length_q = moved_sig.shape[1]
    length_p = 2 * blocks
    total = length_p * length_q
    both = jnp.concatenate([moved_sig, moved_tap], axis=2).transpose(2, 0, 1)
    iota_p = jnp.arange(length_p, dtype=jnp.int32)
    iota_r = jnp.arange(blocks, dtype=jnp.int32)
    iota_q = jnp.arange(length_q, dtype=jnp.int32)
    ang_p = (iota_p[:, None] * iota_r[None, :] % length_p).astype(jnp.float32) * (
        2.0 * math.pi / length_p
    )
    ang_q = (iota_q[:, None] * iota_q[None, :] % length_q).astype(jnp.float32) * (
        2.0 * math.pi / length_q
    )
    ang_t = (iota_p[:, None] * iota_q[None, :] % total).astype(jnp.float32) * (
        2.0 * math.pi / total
    )
    cos_p = jnp.cos(ang_p)
    sin_p = jnp.sin(ang_p)
    cos_q = jnp.cos(ang_q)
    sin_q = jnp.sin(ang_q)
    cos_t = jnp.cos(ang_t)
    sin_t = jnp.sin(ang_t)
    first_re = mixdot("kn,cnq->ckq", cos_p, both)
    first_im = -mixdot("kn,cnq->ckq", sin_p, both)
    tw_re = first_re * cos_t + first_im * sin_t
    tw_im = first_im * cos_t - first_re * sin_t
    spec_re = mixdot("ckq,qm->ckm", tw_re, cos_q) + mixdot("ckq,qm->ckm", tw_im, sin_q)
    spec_im = mixdot("ckq,qm->ckm", tw_im, cos_q) - mixdot("ckq,qm->ckm", tw_re, sin_q)
    half_count = both.shape[0] // 2
    sig_re = spec_re[:half_count]
    sig_im = spec_im[:half_count]
    tap_re = spec_re[half_count:]
    tap_im = spec_im[half_count:]
    prod_re = sig_re * tap_re - sig_im * tap_im
    prod_im = sig_re * tap_im + sig_im * tap_re
    inner_re = mixdot("ckm,mq->ckq", prod_re, cos_q) - mixdot("ckm,mq->ckq", prod_im, sin_q)
    inner_im = mixdot("ckm,mq->ckq", prod_im, cos_q) + mixdot("ckm,mq->ckq", prod_re, sin_q)
    turned_re = inner_re * cos_t - inner_im * sin_t
    turned_im = inner_im * cos_t + inner_re * sin_t
    result = (mixdot("kn,ckq->cnq", cos_p, turned_re) - mixdot("kn,ckq->cnq", sin_p, turned_im)) * (
        1.0 / total
    )
    return lax.all_to_all(
        result.transpose(1, 2, 0).astype(jnp.bfloat16),
        "seq",
        split_axis=1,
        concat_axis=2,
        tiled=True,
    ).astype(jnp.float32)


def body(conv_in, conv_gate, long_filter, skip_gain, queries, keys_in, w_value):
    blocks, slab_rows, channels = conv_in.shape
    my_index = lax.axis_index("seq")
    tokens = blocks * slab_rows
    signal = conv_in.astype(jnp.float32)
    positions = (
        jnp.arange(blocks, dtype=jnp.int32)[:, None] * tokens
        + my_index * slab_rows
        + jnp.arange(slab_rows, dtype=jnp.int32)[None, :]
    )
    convolved = channel_convolve(signal, long_filter)
    mixed = (convolved + skip_gain * signal) * conv_gate.astype(jnp.float32)
    conv_out = mixed.astype(jnp.bfloat16)
    head_size = w_value.shape[1]
    piece = lax.all_gather(conv_out, "chan", axis=2, tiled=True)
    piece_width = piece.shape[2]
    value_sum = jnp.dot(
        piece.reshape(tokens, piece_width), w_value, preferred_element_type=jnp.float32
    )
    values = value_sum.astype(jnp.bfloat16).reshape(blocks, slab_rows, head_size)
    query_rows = queries.reshape(tokens, head_size)
    query_pos = positions.reshape(tokens)
    score_scale = 1.0 / math.sqrt(head_size)
    empty_state = (
        jnp.full((tokens,), -1e30, jnp.float32),
        jnp.zeros((tokens,), jnp.float32),
        jnp.zeros((tokens, head_size), jnp.float32),
    )
    key_piece = lax.all_gather(keys_in, "seq", axis=1, tiled=True)
    value_piece = lax.all_gather(values, "seq", axis=1, tiled=True)
    width_now = key_piece.shape[1]
    target = max(1, 1024 // blocks)
    step_size = 1
    for candidate in range(min(width_now, target), 0, -1):
        step_size = candidate
        break

    def key_step(step_index, current):
        row_best, row_total, row_accum = current
        offset = step_index * step_size
        key_block = lax.dynamic_slice_in_dim(key_piece, offset, step_size, 1).reshape(
            blocks * step_size, head_size
        )
        value_block = lax.dynamic_slice_in_dim(value_piece, offset, step_size, 1).reshape(
            blocks * step_size, head_size
        )
        key_pos = (
            jnp.arange(blocks, dtype=jnp.int32)[:, None] * tokens
            + offset
            + jnp.arange(step_size, dtype=jnp.int32)[None, :]
        ).reshape(blocks * step_size)
        scores = (
            jnp.einsum("qd,kd->qk", query_rows, key_block, preferred_element_type=jnp.float32)
            * score_scale
        )
        allowed = key_pos[None, :] <= query_pos[:, None]
        scores = jnp.where(allowed, scores, -1e30)
        new_best = jnp.maximum(row_best, jnp.max(scores, axis=1))
        factor = jnp.exp(row_best - new_best)
        weights = jnp.where(allowed, jnp.exp(scores - new_best[:, None]), 0.0)
        row_total = row_total * factor + jnp.sum(weights, axis=1)
        row_accum = row_accum * factor[:, None] + jnp.dot(
            weights.astype(jnp.bfloat16), value_block, preferred_element_type=jnp.float32
        )
        return (new_best, row_total, row_accum)

    final_best, final_total, final_accum = lax.fori_loop(
        0, width_now // step_size, key_step, empty_state
    )
    attended = (
        (final_accum / final_total[:, None])
        .astype(jnp.bfloat16)
        .reshape(blocks, slab_rows, head_size)
    )
    return (conv_out, attended)


def solution(mesh):
    return jax.shard_map(
        body,
        mesh=mesh,
        in_specs=(
            P(None, "seq", "chan"),
            P(None, "seq", "chan"),
            P(None, "seq", "chan"),
            P("chan"),
            P(None, "seq", "chan"),
            P(None, "seq", "chan"),
            P(None, "chan"),
        ),
        out_specs=(P(None, "seq", "chan"), P(None, "seq", "chan")),
        check_vma=False,
    )
```

profile of v0, /device:TPU:1, one launch (start us, length us, event | category | flops | bytes accessed | tf_op | source)
XLA Modules:
  0.0 245.0 jit_solution(10891590349229744156)
XLA Ops:
  10.0 8.6 %all-to-all-start.1 = ((bf16[32,2,512]{2,1,0:T(2,128)(2,1)}), bf16[32,2,512]{2,1,0:T(2,128)(2,1)S(1)}, u32[]{:S(2)}, u32[]{:S(2)}) async-start(bf16[32,2,512]{2,1,0:T(2,128)(2,1)} %reshape.130), calls=%async_computation.1 | async-start | bytes 131072 | tf_op jit(solution)/shard_map/all_to_all | solution.py:17
  18.6 1.2 copy.75
  20.7 5.2 %all-to-all-done.1 = bf16[32,2,512]{2,1,0:T(2,128)(2,1)S(1)} async-done(((bf16[32,2,512]{2,1,0:T(2,128)(2,1)}), bf16[32,2,512]{2,1,0:T(2,128)(2,1)S(1)}, u32[]{:S(2)}, u32[]{:S(2)}) %all-to-all-start.1) | async-done | bytes 65568 | tf_op jit(solution)/shard_map/all_to_all | solution.py:17
  26.0 3.9 %all-to-all-start = ((bf16[32,2,512]{2,1,0:T(2,128)(2,1)}), bf16[32,2,512]{2,1,0:T(2,128)(2,1)S(1)}, u32[]{:S(2)}, u32[]{:S(2)}) async-start(bf16[32,2,512]{2,1,0:T(2,128)(2,1)} %reshape.132), calls=%async_computation | async-start | bytes 131072 | tf_op jit(solution)/shard_map/all_to_all | solution.py:14
  30.7 6.6 %all-to-all-done = bf16[32,2,512]{2,1,0:T(2,128)(2,1)S(1)} async-done(((bf16[32,2,512]{2,1,0:T(2,128)(2,1)}), bf16[32,2,512]{2,1,0:T(2,128)(2,1)S(1)}, u32[]{:S(2)}, u32[]{:S(2)}) %all-to-all-start) | async-done | bytes 65568 | tf_op jit(solution)/shard_map/all_to_all | solution.py:14
  38.7 5.4 %fusion.30 = f32[4,64,512]{2,1,0:T(8,128)S(1)} fusion(f32[4,64,512]{2,1,0:T(8,128)S(1)} %convolution_bitcast_fusion, f32[4,64,512]{2,1,0:T(8,128)S(1)} %fusion.15, f32[64,512]{1,0:T(8,128)S(1)} %get-tuple-element.210, f32[64,512]{1,0:T(8,128)S(1)} %get-tuple-element.211), kind=kOutput, calls=%fused_computation.51 | convolution fusion | flops 809369600 | bytes 1835008 | tf_op jit(solution)/shard_map/ckq,qm->ckm/dot_general | solution.py:9
  44.1 5.4 %fusion.32 = f32[4,64,512]{2,1,0:T(8,128)S(1)} fusion(f32[4,64,512]{2,1,0:T(8,128)S(1)} %fusion.15, f32[4,64,512]{2,1,0:T(8,128)S(1)} %convolution_bitcast_fusion, f32[64,512]{1,0:T(8,128)S(1)} %get-tuple-element.210, f32[64,512]{1,0:T(8,128)S(1)} %get-tuple-element.211), kind=kOutput, calls=%fused_computation.53 | convolution fusion | flops 809369600 | bytes 1835008 | tf_op jit(solution)/shard_map/ckq,qm->ckm/dot_general | solution.py:9
  49.5 5.4 %convolution_subtract_fusion = f32[4,64,512]{2,1,0:T(8,128)S(1)} fusion(f32[4,64,512]{2,1,0:T(8,128)S(1)} %fusion.30, f32[4,64,512]{2,1,0:T(8,128)S(1)} %fusion.15, f32[4,64,512]{2,1,0:T(8,128)S(1)} %convolution_bitcast_fusion, f32[64,512]{1,0:T(8,128)S(1)} %get-tuple-element.210, f32[64,512]{1,0:T(8,128)S(1)} %get-tuple-element.211), kind=kOutput, calls=%fused_computation.28 | convolution fusion | flops 809500672 | bytes 2359296 | tf_op jit(solution)/shard_map/ckq,qm->ckm/dot_general | solution.py:9
  54.9 5.6 %convolution_add_fusion.1 = f32[4,64,512]{2,1,0:T(8,128)S(1)} fusion(f32[4,64,512]{2,1,0:T(8,128)S(1)} %fusion.32, f32[4,64,512]{2,1,0:T(8,128)S(1)} %convolution_bitcast_fusion, f32[4,64,512]{2,1,0:T(8,128)S(1)} %fusion.15, f32[64,512]{1,0:T(8,128)S(1)} %get-tuple-element.210, f32[64,512]{1,0:T(8,128)S(1)} %get-tuple-element.211), kind=kOutput, calls=%fused_computation.29 | convolution fusion | flops 809500672 | bytes 2359296 | tf_op jit(solution)/shard_map/ckq,qm->ckm/dot_general | solution.py:9
  60.6 4.9 %fusion.28 = f32[2,64,512]{2,1,0:T(8,128)S(1)} fusion(f32[2,64,512]{2,1,0:T(8,128)S(1)} %get-tuple-element.208), kind=kOutput, calls=%fused_computation.49 | convolution fusion | flops 406323200 | bytes 524288 | tf_op jit(solution)/shard_map/ckm,mq->ckq/dot_general | solution.py:9
  65.5 4.9 %fusion.26 = f32[2,64,512]{2,1,0:T(8,128)S(1)} fusion(f32[2,64,512]{2,1,0:T(8,128)S(1)} %get-tuple-element.209), kind=kOutput, calls=%fused_computation.47 | convolution fusion | flops 406323200 | bytes 524288 | tf_op jit(solution)/shard_map/ckm,mq->ckq/dot_general | solution.py:9
  70.4 4.9 %convolution_subtract_fusion.1 = f32[2,64,512]{2,1,0:T(8,128)S(1)} fusion(f32[2,64,512]{2,1,0:T(8,128)S(1)} %fusion.28, f32[2,64,512]{2,1,0:T(8,128)S(1)} %get-tuple-element.209), kind=kOutput, calls=%fused_computation.34 | convolution fusion | flops 406388736 | bytes 786432 | tf_op jit(solution)/shard_map/ckm,mq->ckq/dot_general | solution.py:9
  75.2 5.1 %convolution_add_fusion.2 = f32[2,64,512]{2,1,0:T(8,128)S(1)} fusion(f32[2,64,512]{2,1,0:T(8,128)S(1)} %fusion.26, f32[2,64,512]{2,1,0:T(8,128)S(1)} %get-tuple-element.208), kind=kOutput, calls=%fused_computation.33 | convolution fusion | flops 406388736 | bytes 786432 | tf_op jit(solution)/shard_map/ckm,mq->ckq/dot_general | solution.py:9
  82.2 3.9 %all-to-all-start.2 = ((bf16[32,2,512]{2,1,0:T(2,128)(2,1)}), bf16[32,2,512]{2,1,0:T(2,128)(2,1)S(1)}, u32[]{:S(2)}, u32[]{:S(2)}) async-start(bf16[32,2,512]{2,1,0:T(2,128)(2,1)} %reshape.134), calls=%async_computation.2 | async-start | bytes 131072 | tf_op jit(solution)/shard_map/all_to_all | solution.py:64
  86.5 7.1 %all-to-all-done.2 = bf16[32,2,512]{2,1,0:T(2,128)(2,1)S(1)} async-done(((bf16[32,2,512]{2,1,0:T(2,128)(2,1)}), bf16[32,2,512]{2,1,0:T(2,128)(2,1)S(1)}, u32[]{:S(2)}, u32[]{:S(2)}) %all-to-all-start.2) | async-done | bytes 65568 | tf_op jit(solution)/shard_map/all_to_all | solution.py:64
  94.1 28.8 %all_gather.10 = bf16[32,16,512]{0,1,2:T(8,128)(2,1)S(1)} all-gather(bf16[32,16,64]{0,1,2:T(8,128)(2,1)S(1)} %fusion.38), channel_id=1, replica_groups=mesh['seq'=32,'chan'=8] {'chan'}, dimensions={2}, use_global_device_ids=true | all-gather | bytes 589824 | tf_op jit(solution)/shard_map/all_gather | solution.py:87
  123.0 2.2 copy.86
  127.2 53.7 %all-gather.5.cloned.1.call-done = bf16[32,512,128]{2,1,0:T(8,128)(2,1)} async-done(((bf16[32,16,128]{2,1,0:T(8,128)(2,1)}), bf16[32,512,128]{2,1,0:T(8,128)(2,1)}) %all-gather.5.cloned.1.call-update) | async-done | bytes 4194320 | tf_op jit(solution)/shard_map/all_gather | solution.py:102
  180.8 56.5 %while.18 = (s32[]{:T(128)}, f32[512]{0:T(512)S(1)}, f32[512]{0:T(512)S(1)}, f32[512,128]{1,0:T(8,128)S(1)}, bf16[32,512,128]{2,1,0:T(8,128)(2,1)}, /*index=5*/b...) while((s32[]{:T(128)}, f32[512]{0:T(512)S(1)}, ...), condition=%wide.region_3.4_spmd.clone, body=%wide.region_0.3_spmd.clone.sunk | while | flops 277024832 | bytes 8589887 | solution.py:139
  181.1 1.1 constant_dynamic-slice_fusion.3
  184.7 1.1 constant_dynamic-slice_fusion.3
  188.2 1.1 constant_dynamic-slice_fusion.3
  191.7 1.1 constant_dynamic-slice_fusion.3
  195.3 1.1 constant_dynamic-slice_fusion.3
  198.8 1.1 constant_dynamic-slice_fusion.3
  202.3 1.1 constant_dynamic-slice_fusion.3
  205.9 1.1 constant_dynamic-slice_fusion.3
  209.4 1.1 constant_dynamic-slice_fusion.3
  212.9 1.1 constant_dynamic-slice_fusion.3
  216.4 1.1 constant_dynamic-slice_fusion.3
  223.5 1.1 constant_dynamic-slice_fusion.3
  234.1 1.1 constant_dynamic-slice_fusion.3
  (223 shorter events, 52.9 us)
Async XLA Ops:
  7.2 118.0 %copy-start = (bf16[512,128]{1,0:T(8,128)(2,1)S(1)}, bf16[512,128]{1,0:T(8,128)(2,1)}, u32[]{:S(2)}) copy-start(bf16[512,128]{1,0:T(8,128)(2,1)} %param.15) | copy-start | bytes 393220
  7.2 120.0 %all-gather.3.cloned.1.call-start = ((), (), s32[]{:S(2)}) async-start(), calls=%async_computation.3 | async-start | bytes 4325376 | tf_op jit(solution)/shard_map/all_gather | solution.py:101
  10.0 15.9 %all-to-all-start.1 = ((bf16[32,2,512]{2,1,0:T(2,128)(2,1)}), bf16[32,2,512]{2,1,0:T(2,128)(2,1)S(1)}, u32[]{:S(2)}, u32[]{:S(2)}) async-start(bf16[32,2,512]{2,1,0:T(2,128)(2,1)} %reshape.130), calls=%async_computation.1 | async-start | bytes 131072 | tf_op jit(solution)/shard_map/all_to_all | solution.py:17
  26.0 11.3 %all-to-all-start = ((bf16[32,2,512]{2,1,0:T(2,128)(2,1)}), bf16[32,2,512]{2,1,0:T(2,128)(2,1)S(1)}, u32[]{:S(2)}, u32[]{:S(2)}) async-start(bf16[32,2,512]{2,1,0:T(2,128)(2,1)} %reshape.132), calls=%async_computation | async-start | bytes 131072 | tf_op jit(solution)/shard_map/all_to_all | solution.py:14
  80.3 5.9 %copy-start.1 = (bf16[32,16,64]{2,1,0:T(8,128)(2,1)S(1)}, bf16[32,16,64]{2,1,0:T(8,128)(2,1)}, u32[]{:S(2)}) copy-start(bf16[32,16,64]{2,1,0:T(8,128)(2,1)} %param.10) | copy-start | bytes 196612
  81.2 12.8 %copy-start.2 = (f32[64]{0:T(128)S(1)}, f32[64]{0:T(128)}, u32[]{:S(2)}) copy-start(f32[64]{0:T(128)} %param.12) | copy-start | bytes 772
  82.2 11.4 %all-to-all-start.2 = ((bf16[32,2,512]{2,1,0:T(2,128)(2,1)}), bf16[32,2,512]{2,1,0:T(2,128)(2,1)S(1)}, u32[]{:S(2)}, u32[]{:S(2)}) async-start(bf16[32,2,512]{2,1,0:T(2,128)(2,1)} %reshape.134), calls=%async_computation.2 | async-start | bytes 131072 | tf_op jit(solution)/shard_map/all_to_all | solution.py:64
  86.2 94.6 %all-gather.5.cloned.1.call-start = ((), (), s32[]{:S(2)}) async-start(), calls=%async_computation.4 | async-start | bytes 4325376 | tf_op jit(solution)/shard_map/all_gather | solution.py:102
  123.0 57.8 %copy-start.3 = (bf16[32,16,128]{2,1,0:T(8,128)(2,1)S(1)}, bf16[32,16,128]{2,1,0:T(8,128)(2,1)}, u32[]{:S(2)}) copy-start(bf16[32,16,128]{2,1,0:T(8,128)(2,1)} %param.13) | copy-start | bytes 393220
Sparse Core Ops, SparseCore 0:
  10.5 58.7 all-gather.2
  126.3 54.5 all-gather.4
where the time goes:
time: 246 us; the launch traced here: 245 us
  waiting for transfers between devices  73.2 us (30%)
  matrix products  67.3 us (27%)
  blocking collectives  28.8 us (12%)
  local copies, waits for them, and re-layouts  28.4 us (12%)
  starting transfers between devices  16.5 us (7%)
  other arithmetic  15.3 us (6%)
  between operations  14.4 us (6%)
    all_gather x1, waiting for transfers between devices, body(): value_piece = lax.all_gather(values, 'seq', axis=1, tiled=True)  53.7 us
    dot_general x12, matrix products, mixdot(): return jnp.einsum(form, left, right, precision=lax.Precision.HIGHEST)  43.3 us
    all_gather x1, blocking collectives, body(): piece = lax.all_gather(conv_out, 'chan', axis=2, tiled=True)  28.8 us
    dynamic_slice x16, local copies, waits for them, and re-layouts, key_step(): lax.dynamic_slice_in_dim(value_piece, offset, step_size, 1)  17.2 us
    dot_general x16, matrix products, key_step(): jnp.dot(weights.astype(jnp.bfloat16), value_block, preferred_element_type...  15.7 us
    reduce_sum x16, other arithmetic, key_step(): row_total = row_total * factor + jnp.sum(weights, axis=1)  9.97 us
    all_to_all x1, starting transfers between devices, channel_convolve(): lax.all_to_all(long_filter.astype(jnp.bfloat16), 'seq', split_axis=2, con...  8.59 us
    dot_general x16, matrix products, key_step(): jnp.einsum('qd,kd->qk', query_rows, key_block, preferred_element_type=jnp...  7.38 us
  transfers between devices with their start and end apart: 5, of which 4 were waited for; matrix products, arithmetic and copies ran while one was open for 22% of the time, Pallas kernels for 0%

commit v1 on v0

--- a/solution.py
+++ b/solution.py
@@ -98,8 +98,11 @@
         jnp.zeros((tokens,), jnp.float32),
         jnp.zeros((tokens, head_size), jnp.float32),
     )
-    key_piece = lax.all_gather(keys_in, "seq", axis=1, tiled=True)
-    value_piece = lax.all_gather(values, "seq", axis=1, tiled=True)
+    key_piece, value_piece = jnp.split(
+        lax.all_gather(jnp.concatenate([keys_in, values], axis=0), "seq", axis=1, tiled=True),
+        [keys_in.shape[0]],
+        axis=0,
+    )
     width_now = key_piece.shape[1]
     target = max(1, 1024 // blocks)
     step_size = 1

time: 246 us -> 261 us (1.061)
  waiting for transfers between devices: 73.2 us -> 82.7 us
  local copies, waits for them, and re-layouts: 28.4 us -> 34.3 us
    all_gather x2 -> x1, waiting for transfers between devices: 53.7 us -> 63.9 us  [body(): lax.all_gather(jnp.concatenate([keys_in, values], axis=0), 'seq', axis=1,...]
    split x0 -> x1, local copies, waits for them, and re-layouts: none -> 5.89 us  [body(): jnp.split(lax.all_gather(jnp.concatenate([keys_in, values], axis=0), 'seq...]
    all_to_all x1, starting transfers between devices: 3.9 us -> 8.59 us  [channel_convolve(): lax.all_to_all(signal.astype(jnp.bfloat16), 'seq', split_axis=2, concat_a...]
    all_to_all x1, starting transfers between devices: 8.59 us -> 3.9 us  [channel_convolve(): lax.all_to_all(long_filter.astype(jnp.bfloat16), 'seq', split_axis=2, con...]
    unnamed x17 -> x19, local copies, waits for them, and re-layouts: 5.61 us -> 5.65 us
  transfers between devices with their start and end apart: 5 -> 4, of which waited for: 4 -> 4; matrix products, arithmetic and copies ran while one was open for 22% -> 2% of each run, Pallas kernels for 0% -> 0%
where the time goes in v1:
time: 261 us; the launch traced here: 260 us
  waiting for transfers between devices  82.7 us (32%)
  matrix products  66.2 us (25%)
  local copies, waits for them, and re-layouts  34.3 us (13%)
  blocking collectives  28.9 us (11%)
  starting transfers between devices  16.4 us (6%)
  other arithmetic  16 us (6%)
  between operations  14.4 us (6%)
    all_gather x1, waiting for transfers between devices, body(): lax.all_gather(jnp.concatenate([keys_in, values], axis=0), 'seq', axis=1,...  63.9 us
    dot_general x12, matrix products, mixdot(): return jnp.einsum(form, left, right, precision=lax.Precision.HIGHEST)  43.3 us
    all_gather x1, blocking collectives, body(): piece = lax.all_gather(conv_out, 'chan', axis=2, tiled=True)  28.9 us
    dynamic_slice x16, local copies, waits for them, and re-layouts, key_step(): lax.dynamic_slice_in_dim(value_piece, offset, step_size, 1)  17.3 us
    dot_general x16, matrix products, key_step(): jnp.dot(weights.astype(jnp.bfloat16), value_block, preferred_element_type...  15.1 us
    reduce_sum x16, other arithmetic, key_step(): row_total = row_total * factor + jnp.sum(weights, axis=1)  9.95 us
    all_to_all x1, starting transfers between devices, channel_convolve(): lax.all_to_all(signal.astype(jnp.bfloat16), 'seq', split_axis=2, concat_a...  8.59 us
    dot_general x16, matrix products, key_step(): jnp.einsum('qd,kd->qk', query_rows, key_block, preferred_element_type=jnp...  7.47 us
  transfers between devices with their start and end apart: 4, of which 4 were waited for; matrix products, arithmetic and copies ran while one was open for 2% of the time, Pallas kernels for 0%

profile of v1, /device:TPU:1, one launch (start us, length us, event | category | flops | bytes accessed | tf_op | source)
XLA Modules:
  0.0 260.0 jit_solution(16652453829377808419)
XLA Ops:
  7.2 1.2 copy.75
  9.3 8.6 %all-to-all-start = ((bf16[32,2,512]{2,1,0:T(2,128)(2,1)}), bf16[32,2,512]{2,1,0:T(2,128)(2,1)S(1)}, u32[]{:S(2)}, u32[]{:S(2)}) async-start(bf16[32,2,512]{2,1,0:T(2,128)(2,1)} %reshape.132), calls=%async_computation | async-start | bytes 131072 | tf_op jit(solution)/shard_map/all_to_all | solution.py:14
  20.0 5.2 %all-to-all-done = bf16[32,2,512]{2,1,0:T(2,128)(2,1)S(1)} async-done(((bf16[32,2,512]{2,1,0:T(2,128)(2,1)}), bf16[32,2,512]{2,1,0:T(2,128)(2,1)S(1)}, u32[]{:S(2)}, u32[]{:S(2)}) %all-to-all-start) | async-done | bytes 65568 | tf_op jit(solution)/shard_map/all_to_all | solution.py:14
  25.2 3.9 %all-to-all-start.1 = ((bf16[32,2,512]{2,1,0:T(2,128)(2,1)}), bf16[32,2,512]{2,1,0:T(2,128)(2,1)S(1)}, u32[]{:S(2)}, u32[]{:S(2)}) async-start(bf16[32,2,512]{2,1,0:T(2,128)(2,1)} %reshape.130), calls=%async_computation.1 | async-start | bytes 131072 | tf_op jit(solution)/shard_map/all_to_all | solution.py:17
  30.0 6.6 %all-to-all-done.1 = bf16[32,2,512]{2,1,0:T(2,128)(2,1)S(1)} async-done(((bf16[32,2,512]{2,1,0:T(2,128)(2,1)}), bf16[32,2,512]{2,1,0:T(2,128)(2,1)S(1)}, u32[]{:S(2)}, u32[]{:S(2)}) %all-to-all-start.1) | async-done | bytes 65568 | tf_op jit(solution)/shard_map/all_to_all | solution.py:17
  37.9 5.4 %fusion.32 = f32[4,64,512]{2,1,0:T(8,128)S(1)} fusion(f32[4,64,512]{2,1,0:T(8,128)S(1)} %fusion.15, f32[4,64,512]{2,1,0:T(8,128)S(1)} %convolution_bitcast_fusion, f32[64,512]{1,0:T(8,128)S(1)} %get-tuple-element.212, f32[64,512]{1,0:T(8,128)S(1)} %get-tuple-element.213), kind=kOutput, calls=%fused_computation.53 | convolution fusion | flops 809369600 | bytes 1835008 | tf_op jit(solution)/shard_map/ckq,qm->ckm/dot_general | solution.py:9
  43.3 5.4 %fusion.30 = f32[4,64,512]{2,1,0:T(8,128)S(1)} fusion(f32[4,64,512]{2,1,0:T(8,128)S(1)} %convolution_bitcast_fusion, f32[4,64,512]{2,1,0:T(8,128)S(1)} %fusion.15, f32[64,512]{1,0:T(8,128)S(1)} %get-tuple-element.212, f32[64,512]{1,0:T(8,128)S(1)} %get-tuple-element.213), kind=kOutput, calls=%fused_computation.51 | convolution fusion | flops 809369600 | bytes 1835008 | tf_op jit(solution)/shard_map/ckq,qm->ckm/dot_general | solution.py:9
  48.8 5.4 %convolution_add_fusion.1 = f32[4,64,512]{2,1,0:T(8,128)S(1)} fusion(f32[4,64,512]{2,1,0:T(8,128)S(1)} %fusion.32, f32[4,64,512]{2,1,0:T(8,128)S(1)} %convolution_bitcast_fusion, f32[4,64,512]{2,1,0:T(8,128)S(1)} %fusion.15, f32[64,512]{1,0:T(8,128)S(1)} %get-tuple-element.212, f32[64,512]{1,0:T(8,128)S(1)} %get-tuple-element.213), kind=kOutput, calls=%fused_computation.29 | convolution fusion | flops 809500672 | bytes 2359296 | tf_op jit(solution)/shard_map/ckq,qm->ckm/dot_general | solution.py:9
  54.2 5.6 %convolution_subtract_fusion = f32[4,64,512]{2,1,0:T(8,128)S(1)} fusion(f32[4,64,512]{2,1,0:T(8,128)S(1)} %fusion.30, f32[4,64,512]{2,1,0:T(8,128)S(1)} %fusion.15, f32[4,64,512]{2,1,0:T(8,128)S(1)} %convolution_bitcast_fusion, f32[64,512]{1,0:T(8,128)S(1)} %get-tuple-element.212, f32[64,512]{1,0:T(8,128)S(1)} %get-tuple-element.213), kind=kOutput, calls=%fused_computation.28 | convolution fusion | flops 809500672 | bytes 2359296 | tf_op jit(solution)/shard_map/ckq,qm->ckm/dot_general | solution.py:9
  59.9 4.9 %fusion.28 = f32[2,64,512]{2,1,0:T(8,128)S(1)} fusion(f32[2,64,512]{2,1,0:T(8,128)S(1)} %get-tuple-element.210), kind=kOutput, calls=%fused_computation.49 | convolution fusion | flops 406323200 | bytes 524288 | tf_op jit(solution)/shard_map/ckm,mq->ckq/dot_general | solution.py:9
  64.8 4.9 %fusion.26 = f32[2,64,512]{2,1,0:T(8,128)S(1)} fusion(f32[2,64,512]{2,1,0:T(8,128)S(1)} %get-tuple-element.211), kind=kOutput, calls=%fused_computation.47 | convolution fusion | flops 406323200 | bytes 524288 | tf_op jit(solution)/shard_map/ckm,mq->ckq/dot_general | solution.py:9
  69.6 4.9 %convolution_subtract_fusion.1 = f32[2,64,512]{2,1,0:T(8,128)S(1)} fusion(f32[2,64,512]{2,1,0:T(8,128)S(1)} %fusion.28, f32[2,64,512]{2,1,0:T(8,128)S(1)} %get-tuple-element.211), kind=kOutput, calls=%fused_computation.34 | convolution fusion | flops 406388736 | bytes 786432 | tf_op jit(solution)/shard_map/ckm,mq->ckq/dot_general | solution.py:9
  74.5 5.1 %convolution_add_fusion.2 = f32[2,64,512]{2,1,0:T(8,128)S(1)} fusion(f32[2,64,512]{2,1,0:T(8,128)S(1)} %fusion.26, f32[2,64,512]{2,1,0:T(8,128)S(1)} %get-tuple-element.210), kind=kOutput, calls=%fused_computation.33 | convolution fusion | flops 406388736 | bytes 786432 | tf_op jit(solution)/shard_map/ckm,mq->ckq/dot_general | solution.py:9
  81.5 3.9 %all-to-all-start.2 = ((bf16[32,2,512]{2,1,0:T(2,128)(2,1)}), bf16[32,2,512]{2,1,0:T(2,128)(2,1)S(1)}, u32[]{:S(2)}, u32[]{:S(2)}) async-start(bf16[32,2,512]{2,1,0:T(2,128)(2,1)} %reshape.134), calls=%async_computation.2 | async-start | bytes 131072 | tf_op jit(solution)/shard_map/all_to_all | solution.py:64
  85.8 7.1 %all-to-all-done.2 = bf16[32,2,512]{2,1,0:T(2,128)(2,1)S(1)} async-done(((bf16[32,2,512]{2,1,0:T(2,128)(2,1)}), bf16[32,2,512]{2,1,0:T(2,128)(2,1)S(1)}, u32[]{:S(2)}, u32[]{:S(2)}) %all-to-all-start.2) | async-done | bytes 65568 | tf_op jit(solution)/shard_map/all_to_all | solution.py:64
  93.4 28.9 %all_gather.6 = bf16[32,16,512]{0,1,2:T(8,128)(2,1)S(1)} all-gather(bf16[32,16,64]{0,1,2:T(8,128)(2,1)S(1)} %fusion.38), channel_id=1, replica_groups=mesh['seq'=32,'chan'=8] {'chan'}, dimensions={2}, use_global_device_ids=true | all-gather | bytes 589824 | tf_op jit(solution)/shard_map/all_gather | solution.py:87
  122.3 2.2 copy.86
  126.6 63.9 %all-gather.2.cloned.1.call-done = bf16[64,512,128]{2,1,0:T(8,128)(2,1)} async-done(((bf16[64,16,128]{2,1,0:T(8,128)(2,1)}), bf16[64,512,128]{2,1,0:T(8,128)(2,1)}) %all-gather.2.cloned.1.call-update) | async-done | bytes 8388624 | tf_op jit(solution)/shard_map/all_gather | solution.py:102
  190.4 5.9 %fusion.134 = (bf16[32,512,128]{2,1,0:T(8,128)(2,1)}, bf16[32,512,128]{2,1,0:T(8,128)(2,1)}) fusion(bf16[64,512,128]{2,1,0:T(8,128)(2,1)} %all-gather.2.cloned.1.call-done), kind=kLoop, calls=%fused_computation.159 | loop fusion | bytes 16777216 | tf_op jit(solution)/shard_map/split | solution.py:101
  196.3 56.0 %while.18 = (s32[]{:T(128)}, f32[512]{0:T(512)S(1)}, f32[512]{0:T(512)S(1)}, f32[512,128]{1,0:T(8,128)S(1)}, bf16[32,512,128]{2,1,0:T(8,128)(2,1)}, /*index=5*/b...) while((s32[]{:T(128)}, f32[512]{0:T(512)S(1)}, ...), condition=%wide.region_3.4_spmd.clone, body=%wide.region_0.3_spmd.clone.sunk | while | flops 277024832 | bytes 8589879 | solution.py:142
  199.8 1.1 constant_dynamic-slice_fusion.3
  203.3 1.1 constant_dynamic-slice_fusion.3
  206.8 1.1 constant_dynamic-slice_fusion.3
  210.3 1.1 constant_dynamic-slice_fusion.3
  213.8 1.1 constant_dynamic-slice_fusion.3
  217.4 1.1 constant_dynamic-slice_fusion.3
  220.9 1.1 constant_dynamic-slice_fusion.3
  224.4 1.1 constant_dynamic-slice_fusion.3
  227.9 1.1 constant_dynamic-slice_fusion.3
  231.4 1.1 constant_dynamic-slice_fusion.3
  234.9 1.1 constant_dynamic-slice_fusion.3
  238.4 1.1 constant_dynamic-slice_fusion.3
  (224 shorter events, 52.8 us)
Async XLA Ops:
  7.2 117.3 %copy-start = (bf16[512,128]{1,0:T(8,128)(2,1)S(1)}, bf16[512,128]{1,0:T(8,128)(2,1)}, u32[]{:S(2)}) copy-start(bf16[512,128]{1,0:T(8,128)(2,1)} %param.15) | copy-start | bytes 393220
  9.3 15.9 %all-to-all-start = ((bf16[32,2,512]{2,1,0:T(2,128)(2,1)}), bf16[32,2,512]{2,1,0:T(2,128)(2,1)S(1)}, u32[]{:S(2)}, u32[]{:S(2)}) async-start(bf16[32,2,512]{2,1,0:T(2,128)(2,1)} %reshape.132), calls=%async_computation | async-start | bytes 131072 | tf_op jit(solution)/shard_map/all_to_all | solution.py:14
  25.2 11.3 %all-to-all-start.1 = ((bf16[32,2,512]{2,1,0:T(2,128)(2,1)}), bf16[32,2,512]{2,1,0:T(2,128)(2,1)S(1)}, u32[]{:S(2)}, u32[]{:S(2)}) async-start(bf16[32,2,512]{2,1,0:T(2,128)(2,1)} %reshape.130), calls=%async_computation.1 | async-start | bytes 131072 | tf_op jit(solution)/shard_map/all_to_all | solution.py:17
  79.6 5.9 %copy-start.1 = (bf16[32,16,64]{2,1,0:T(8,128)(2,1)S(1)}, bf16[32,16,64]{2,1,0:T(8,128)(2,1)}, u32[]{:S(2)}) copy-start(bf16[32,16,64]{2,1,0:T(8,128)(2,1)} %param.10) | copy-start | bytes 196612
  80.5 12.7 %copy-start.3 = (f32[64]{0:T(128)S(1)}, f32[64]{0:T(128)}, u32[]{:S(2)}) copy-start(f32[64]{0:T(128)} %param.12) | copy-start | bytes 772
  81.5 11.3 %all-to-all-start.2 = ((bf16[32,2,512]{2,1,0:T(2,128)(2,1)}), bf16[32,2,512]{2,1,0:T(2,128)(2,1)S(1)}, u32[]{:S(2)}, u32[]{:S(2)}) async-start(bf16[32,2,512]{2,1,0:T(2,128)(2,1)} %reshape.134), calls=%async_computation.2 | async-start | bytes 131072 | tf_op jit(solution)/shard_map/all_to_all | solution.py:64
  85.4 105.0 %all-gather.2.cloned.1.call-start = ((), (), s32[]{:S(2)}) async-start(), calls=%async_computation.3 | async-start | bytes 8650752 | tf_op jit(solution)/shard_map/all_gather | solution.py:102
  122.3 2.5 copy-start.2
  126.6 69.8 %copy-start.4 = (bf16[32,16,128]{2,1,0:T(8,128)(2,1)S(1)}, bf16[32,16,128]{2,1,0:T(8,128)(2,1)}, u32[]{:S(2)}) copy-start(bf16[32,16,128]{2,1,0:T(8,128)(2,1)} %param.13) | copy-start | bytes 393220
Sparse Core Ops, SparseCore 0:
  125.7 64.7 all-gather.1
